TPU v7x, 256 devices: a whole 4x4x8 slice. The times are simulated.
256 devices in a mesh: row: 4 (over x), col: 16 (over y_hi, z), pair: 4 (over y_lo, core).
Axes of the slice: x: 4, y: 4 (y_hi: 2, y_lo: 2; y = y_hi * 2 + y_lo), z: 8, core: 2. Of those that a mesh axis runs over, the one named last changes fastest.
Arguments:
- frames: bfloat16 [4, 2, 64, 512, 256], P('pair', None, 'row', 'col'), may hold values from -6 to 6
- offsets: int32 [4, 2, 16, 2], P('pair'), may hold values from -8 to 8, as said below
- weight: bfloat16 [3, 3, 256, 256], replicated, may hold values from -0.125 to 0.125
- bias: float32 [256], replicated, may hold values from -3 to 3
- cotangent: bfloat16 [4, 81, 64, 512], P('pair', None, 'row', 'col'), may hold values from -0.023925781 to 0.023925781
Outputs:
- corr: bfloat16 [4, 81, 64, 512], P('pair', None, 'row', 'col')
- grad_weight: float32 [3, 3, 256, 256], replicated
- grad_bias: float32 [256], replicated
Inputs may be any that keep to these rules, and one draw needn't show every extreme that they name: `offsets`: entry [.., 0] shifts rows and [.., 1] columns of one 32 x 32 block; both ends of the range occur in every draw.
All inputs are finite; a program needn't handle non-finite values.
Results may differ from a plain program's by a relative error of at most 0.0046.
Values may be sent and summed in bfloat16 or wider, within the bound.
No kernel may reach another device: no remote copies, remote signals or barrier semaphores. Data moves between devices by JAX's collectives and lax.ppermute only.
A program may use at most 64 MiB of HBM per device.

v0:
```python
import jax
import jax.numpy as jnp
from jax import lax
from jax.sharding import PartitionSpec as P

BLK = 32
RAD = 4
MAXOFF = 8


def with_halo(cells, sides, width):
    for axis, dim in sides:
        count = lax.axis_size(axis)
        ends = count - 1
        head = lax.slice_in_dim(cells, 0, width, axis=dim)
        tail = lax.slice_in_dim(cells, cells.shape[dim] - width, cells.shape[dim], axis=dim)
        cells = jnp.concatenate(
            [
                lax.ppermute(tail, axis, [(i, (i + 1) % count) for i in range(ends)]),
                cells,
                lax.ppermute(head, axis, [((i + 1) % count, i) for i in range(ends)]),
            ],
            axis=dim,
        )
    return cells


def band_take(scores):
    row_count, col_count, patch_width = scores.shape
    widened = jnp.pad(scores, ((0, 0), (0, 0), (0, 1)))
    flattened = widened.reshape(row_count, col_count * (patch_width + 1))
    flattened = jnp.pad(flattened, ((0, 0), (0, col_count)))
    return flattened.reshape(row_count, col_count, patch_width + 2)[:, :, : 2 * RAD + 1]


def band_spread(bands, patch_width):
    row_count, col_count, window_size = bands.shape
    widened = jnp.pad(bands, ((0, 0), (0, 0), (0, patch_width + 2 - window_size)))
    flattened = widened.reshape(row_count, col_count * (patch_width + 2))[
        :, : col_count * (patch_width + 1)
    ]
    return flattened.reshape(row_count, col_count, patch_width + 1)[:, :, :patch_width]


def block_scores(block_one, window_two):
    row_count, col_count = (block_one.shape[0], block_one.shape[1])
    window_size = 2 * RAD + 1
    score_list = []
    for row_shift in range(window_size):
        scores = jnp.einsum(
            "yxc,yzc->yxz",
            block_one,
            window_two[row_shift : row_shift + row_count],
            preferred_element_type=jnp.float32,
        )
        score_list.append(band_take(scores))
    stacked = jnp.stack(score_list)
    return jnp.transpose(stacked, (0, 3, 1, 2)).reshape(
        window_size * window_size, row_count, col_count
    )


def block_grads(cot_block, block_one, window_two):
    row_count, col_count, channels = block_one.shape
    window_size = 2 * RAD + 1
    patch_width = col_count + 2 * RAD
    cot_grid = jnp.transpose(
        cot_block.reshape(window_size, window_size, row_count, col_count), (0, 2, 3, 1)
    )
    grad_block = jnp.zeros((row_count, col_count, channels), jnp.float32)
    grad_window = jnp.zeros((row_count + 2 * RAD, patch_width, channels), jnp.float32)
    for row_shift in range(window_size):
        spread = band_spread(cot_grid[row_shift], patch_width)
        grad_block = grad_block + jnp.einsum(
            "yxz,yzc->yxc",
            spread,
            window_two[row_shift : row_shift + row_count],
            preferred_element_type=jnp.float32,
        )
        patch_term = jnp.einsum(
            "yxz,yxc->yzc", spread, block_one, preferred_element_type=jnp.float32
        )
        grad_window = grad_window.at[row_shift : row_shift + row_count].add(patch_term)
    return (grad_block, grad_window)


def convolve(padded, weight, bias, row_count, col_count):
    channels = weight.shape[3]
    accumulated = jnp.zeros((row_count * col_count, channels), jnp.float32)
    for tap_row in range(3):
        for tap_col in range(3):
            window = padded[tap_row : tap_row + row_count, tap_col : tap_col + col_count].reshape(
                row_count * col_count, -1
            )
            accumulated = accumulated + jnp.dot(
                window, weight[tap_row, tap_col], preferred_element_type=jnp.float32
            )
    return accumulated.reshape(row_count, col_count, channels) + bias


def weight_terms(padded, delta, input_float):
    row_count, col_count, channels = delta.shape
    flat_delta = delta.reshape(row_count * col_count, channels)
    tap_list = []
    for tap_row in range(3):
        for tap_col in range(3):
            window = padded[tap_row : tap_row + row_count, tap_col : tap_col + col_count].reshape(
                row_count * col_count, -1
            )
            if input_float:
                tap_list.append(
                    jnp.einsum(
                        "pc,pd->cd",
                        window.astype(jnp.float32),
                        flat_delta,
                        precision=lax.Precision.HIGHEST,
                    )
                )
            else:
                tap_list.append(
                    jnp.einsum("pc,pd->cd", window, flat_delta, preferred_element_type=jnp.float32)
                )
    return jnp.stack(tap_list).reshape(3, 3, channels, channels)


def shards(frames, offsets, weight, bias, cotangent):
    tile_rows, tile_cols, channels = (frames.shape[2], frames.shape[3], frames.shape[4])
    border_width = MAXOFF + RAD
    row_start = lax.axis_index("row") * tile_rows
    col_start = lax.axis_index("col") * tile_cols
    inv_root = channels ** (-0.5)
    bordered = with_halo(frames, (("row", 2), ("col", 3)), 1)
    first_pad = bordered[0, 0]
    second_pad = bordered[0, 1]
    pre_one = convolve(first_pad, weight, bias, tile_rows, tile_cols)
    pre_two = convolve(second_pad, weight, bias, tile_rows, tile_cols)
    feat_two = jnp.maximum(pre_two, 0.0).astype(jnp.bfloat16)
    padded_two = with_halo(feat_two, (("row", 0), ("col", 1)), border_width)
    feat_one = jnp.maximum(pre_one, 0.0).astype(jnp.bfloat16)
    sub_rows = min(tile_rows, BLK)
    gradient_second_padded = jnp.zeros(
        (tile_rows + 2 * border_width, tile_cols + 2 * border_width, channels), jnp.float32
    )
    zero_index = jnp.zeros((), jnp.int32)
    block_row = (row_start + 0) // BLK
    block_col = (col_start + 0) // BLK
    shift_pair = offsets[0, block_row, block_col]
    start = (0 + shift_pair[0] + MAXOFF, 0 + shift_pair[1] + MAXOFF, zero_index)
    window_two = lax.dynamic_slice(padded_two, start, (sub_rows + 2 * RAD, BLK + 2 * RAD, channels))
    corr_pieces = block_scores(feat_one, window_two) * inv_root
    cot_block = cotangent[0, :, 0:sub_rows, 0:BLK]
    grad_block, grad_window = block_grads(cot_block, feat_one, window_two)
    grad_pieces = grad_block * inv_root
    gradient_second_padded = lax.dynamic_update_slice(
        gradient_second_padded, grad_window * inv_root, start
    )
    corr = corr_pieces.astype(jnp.bfloat16)[None]
    carried_state = jnp.concatenate(
        [gradient_second_padded[:border_width], gradient_second_padded[-border_width:]], axis=0
    )
    incoming_block = with_halo(
        carried_state.astype(jnp.bfloat16), (("row", 0),), border_width
    ).astype(carried_state.dtype)
    central_index = gradient_second_padded[border_width : border_width + tile_rows]
    central_index = central_index.at[:border_width].add(incoming_block[:border_width])
    central_index = central_index.at[tile_rows - border_width :].add(
        incoming_block[3 * border_width :]
    )
    carried_state = jnp.concatenate(
        [central_index[:, :border_width], central_index[:, -border_width:]], axis=1
    )
    incoming_block = with_halo(
        carried_state.astype(jnp.bfloat16), (("col", 1),), border_width
    ).astype(carried_state.dtype)
    center = central_index[:, border_width : border_width + tile_cols]
    center = center.at[:, :border_width].add(incoming_block[:, :border_width])
    center = center.at[:, tile_cols - border_width :].add(incoming_block[:, 3 * border_width :])
    delta_two = jnp.where(pre_two > 0, center, 0.0)
    delta_one = jnp.where(pre_one > 0, grad_pieces, 0.0).astype(jnp.bfloat16)
    grad_w = weight_terms(first_pad, delta_one, False) + weight_terms(second_pad, delta_two, True)
    grad_b = jnp.sum(delta_one.astype(jnp.float32), axis=(0, 1)) + jnp.sum(delta_two, axis=(0, 1))
    grad_w, grad_b = lax.psum((grad_w, grad_b), ("row", "col", "pair"))
    return (corr, grad_w, grad_b)


def solution(mesh):
    return jax.shard_map(
        shards,
        mesh=mesh,
        in_specs=(
            P("pair", None, "row", "col", None),
            P("pair", None, None, None),
            P(),
            P(),
            P("pair", None, "row", "col"),
        ),
        out_specs=(P("pair", None, "row", "col"), P(), P()),
        check_vma=False,
    )
```

profile of v0, /device:TPU:2, one launch (start us, length us, event | category | flops | bytes accessed | tf_op | source)
XLA Modules:
  0.0 393.6 jit_solution(6452110076248892458)
XLA Ops:
  7.2 0.8 fusion.142
  8.0 3.4 collective-permute-start
  11.4 2.4 collective-permute-start.1
  13.9 1.2 copy.31
  15.3 1.1 constant_dynamic-update-slice_fusion.1
  16.3 0.9 collective-permute-done.1
  17.3 3.8 collective-permute-start.2
  21.1 1.3 collective-permute-start.3
  22.4 0.5 fusion.147
  23.4 0.3 reshape.635
  24.2 0.3 reshape.637
  25.0 0.3 reshape.639
  25.8 0.3 reshape.641
  26.6 0.3 reshape.643
  27.4 0.3 reshape.645
  28.2 0.3 reshape.647
  29.0 0.3 reshape.649
  29.8 0.3 reshape.651
  32.8 0.4 pad_maximum_fusion
  33.3 1.6 fusion.144
  35.0 1.1 fusion.79
  38.2 0.7 copy-done.1
  40.0 0.3 fusion.5
  40.3 0.3 fusion.4
  40.7 0.3 fusion.3
  41.0 0.3 fusion.2
  41.3 0.3 fusion.1
  42.0 1.0 broadcast_multiply_fusion
  43.1 9.8 %dynamic_update_slice.3 = f32[40,56,256]{2,1,0:T(8,128)S(1)} dynamic-update-slice(f32[40,56,256]{2,1,0:T(8,128)S(1)} %broadcast_in_dim.4, f32[24,40,256]{2,1,0:T(8,128)} %broadcast_multiply_fusion, s32[]{:T(128)S(6)} %select_n.33, s32[]{:T(128)S(6)} %select_n.34, s32[]{:T(128)} %constant.386.clone.1) | dynamic-update-slice | bytes 1966084 | tf_op jit(solution)/shard_map/dynamic_update_slice | solution.py:154
  53.2 3.0 collective-permute-start.8
  56.2 3.2 collective-permute-start.9
  61.2 0.4 copy-done.24
  61.8 1.3 collective-permute-done.8
  63.1 2.4 collective-permute-done.9
  65.9 5.4 %collective-permute-start.10 = (bf16[16,12,256]{2,1,0:T(8,128)(2,1)S(1)}, bf16[16,12,256]{2,1,0:T(8,128)(2,1)S(1)}, u32[]{:S(2)}, u32[]{:S(2)}) collective-permute-start(bf16[16,12,256]{2,1,0:T(8,128)(2,1)S(1)} %get-tuple-element.181), channel_id=1, source_target_pairs={{0,4},{4,8},{8,12},{12,16},{16,20},{20,24},{24,28},{28,32},{32,36}... | collective-permute-start | bytes 294920 | tf_op jit(solution)/shard_map/ppermute | solution.py:19
  71.3 1.3 collective-permute-start.11
  72.9 0.9 collective-permute-done.10
  73.8 4.4 %collective-permute-done.11 = bf16[16,12,256]{2,1,0:T(8,128)(2,1)S(1)} collective-permute-done((bf16[16,12,256]{2,1,0:T(8,128)(2,1)S(1)}, bf16[16,12,256]{2,1,0:T(8,128)(2,1)S(1)}, u32[]{:S(2)}, u32[]{:S(2)}) %collective-permute-start.11) | collective-permute-done | bytes 98336 | tf_op jit(solution)/shard_map/ppermute | solution.py:21
  78.2 0.4 scatter-add.61
  78.7 0.3 scatter-add.64
  79.2 3.1 collective-permute-start.4
  82.3 2.8 collective-permute-start.5
  85.1 0.5 fusion.19
  85.6 0.5 fusion.18
  86.1 0.5 fusion.17
  86.6 0.5 fusion.16
  87.1 0.5 fusion.15
  87.6 0.5 fusion.14
  88.1 0.5 fusion.13
  88.6 0.5 fusion.12
  89.1 0.8 collective-permute-done.5
  90.1 4.7 %collective-permute-start.6 = (bf16[40,12,256]{2,1,0:T(8,128)(2,1)S(1)}, bf16[40,12,256]{2,1,0:T(8,128)(2,1)S(1)}, u32[]{:S(2)}, u32[]{:S(2)}) collective-permute-start(bf16[40,12,256]{2,1,0:T(8,128)(2,1)S(1)} %get-tuple-element.175), channel_id=1, source_target_pairs={{0,4},{4,8},{8,12},{12,16},{16,20},{20,24},{24,28},{28,32},{32,36}... | collective-permute-start | bytes 737288 | tf_op jit(solution)/shard_map/ppermute | solution.py:19
  94.8 1.3 collective-permute-start.7
  96.1 0.5 fusion.11
  96.6 2.7 collective-permute-done.6
  99.4 5.5 %collective-permute-done.7 = bf16[40,12,256]{2,1,0:T(8,128)(2,1)S(1)} collective-permute-done((bf16[40,12,256]{2,1,0:T(8,128)(2,1)S(1)}, bf16[40,12,256]{2,1,0:T(8,128)(2,1)S(1)}, u32[]{:S(2)}, u32[]{:S(2)}) %collective-permute-start.7) | collective-permute-done | bytes 245792 | tf_op jit(solution)/shard_map/ppermute | solution.py:21
  104.8 1.4 fusion.32
  106.4 0.9 fusion.39
  114.2 1.7 add.331
  115.9 0.9 copy-done.22
  123.5 1.0 copy.41
  124.5 82.2 %psum.15 = f32[256]{0:T(256)} all-reduce(f32[256]{0:T(256)S(1)} %add.333), channel_id=1, replica_groups=mesh['row'=4,'col'=16,'pair'=4] {'row','col','pair'}, use_global_device_ids=true, to_apply=%region_3.4 | all-reduce | flops 256 | bytes 2048 | tf_op jit(solution)/shard_map/psum | solution.py:182
  206.6 176.9 %all-reduce.30.cloned.1.call-done = f32[3,3,256,256]{3,2,1,0:T(8,128)} async-done(((f32[3,3,256,256]{3,2,1,0:T(8,128)}), f32[3,3,256,256]{3,2,1,0:T(8,128)}) %all-reduce.30.cloned.1.call-update) | async-done | bytes 2359312 | tf_op jit(solution)/shard_map/psum | solution.py:182
  383.6 3.2 copy.91
  (229 shorter events, 24.1 us)
Async XLA Ops:
  7.2 8.0 %copy-start = (s32[1,2,16,2]{2,3,1,0:T(2,128)S(1)}, s32[1,2,16,2]{2,3,1,0:T(2,128)}, u32[]{:S(2)}) copy-start(s32[1,2,16,2]{2,3,1,0:T(2,128)} %param.32) | copy-start | bytes 772
  7.2 376.4 %all-reduce.30.cloned.1.call-start = ((), (), s32[]{:S(2)}) async-start(), calls=%async_computation | async-start | bytes 4718592 | tf_op jit(solution)/shard_map/psum | solution.py:182
  8.0 7.2 %collective-permute-start = (bf16[1,2,1,32,256]{4,3,2,1,0:T(8,128)(2,1)S(1)}, bf16[1,2,1,32,256]{4,3,2,1,0:T(8,128)(2,1)S(1)}, u32[]{:S(2)}, u32[]{:S(2)}) collective-permute-start(bf16[1,2,1,32,256]{4,3,2,1,0:T(8,128)(2,1)S(1)} %get-tuple-element.180), channel_id=1, source_target_pairs={{0,64},{64,128},{128,192},{1,65},{65,129},{129,193},{2,66},{66,130... | collective-permute-start | bytes 98312 | tf_op jit(solution)/shard_map/ppermute | solution.py:19
  11.4 5.8 %collective-permute-start.1 = (bf16[1,2,1,32,256]{4,3,2,1,0:T(8,128)(2,1)S(1)}, bf16[1,2,1,32,256]{4,3,2,1,0:T(8,128)(2,1)S(1)}, u32[]{:S(2)}, u32[]{:S(2)}) collective-permute-start(bf16[1,2,1,32,256]{4,3,2,1,0:T(8,128)(2,1)S(1)} %get-tuple-element.179), channel_id=1, source_target_pairs={{64,0},{128,64},{192,128},{65,1},{129,65},{193,129},{66,2},{130,66... | collective-permute-start | bytes 98312 | tf_op jit(solution)/shard_map/ppermute | solution.py:21
  17.3 15.5 %collective-permute-start.2 = (bf16[1,2,18,1,256]{4,3,2,1,0:T(2,128)(2,1)S(1)}, bf16[1,2,18,1,256]{4,3,2,1,0:T(2,128)(2,1)S(1)}, u32[]{:S(2)}, u32[]{:S(2)}) collective-permute-start(bf16[1,2,18,1,256]{4,3,2,1,0:T(2,128)(2,1)S(1)} %get-tuple-element.176), channel_id=1, source_target_pairs={{0,4},{4,8},{8,12},{12,16},{16,20},{20,24},{24,28},{28,32},{32,36}... | collective-permute-start | bytes 55304 | tf_op jit(solution)/shard_map/ppermute | solution.py:19
  21.1 11.6 %collective-permute-start.3 = (bf16[1,2,18,1,256]{4,3,2,1,0:T(2,128)(2,1)S(1)}, bf16[1,2,18,1,256]{4,3,2,1,0:T(2,128)(2,1)S(1)}, u32[]{:S(2)}, u32[]{:S(2)}) collective-permute-start(bf16[1,2,18,1,256]{4,3,2,1,0:T(2,128)(2,1)S(1)} %get-tuple-element.177), channel_id=1, source_target_pairs={{4,0},{8,4},{12,8},{16,12},{20,16},{24,20},{28,24},{32,28},{36,32}... | collective-permute-start | bytes 55304 | tf_op jit(solution)/shard_map/ppermute | solution.py:21
  24.5 14.8 %copy-start.10 = (bf16[16,32,41]{2,1,0:T(8,128)(2,1)}, bf16[16,32,41]{2,1,0:T(8,128)(2,1)S(1)}, u32[]{:S(2)}) copy-start(bf16[16,32,41]{2,1,0:T(8,128)(2,1)S(1)} %reshape.637) | copy-start | bytes 125956
  25.3 14.3 %copy-start.6 = (bf16[16,32,41]{2,1,0:T(8,128)(2,1)}, bf16[16,32,41]{2,1,0:T(8,128)(2,1)S(1)}, u32[]{:S(2)}) copy-start(bf16[16,32,41]{2,1,0:T(8,128)(2,1)S(1)} %reshape.639) | copy-start | bytes 125956
  26.1 13.9 %copy-start.8 = (bf16[16,32,41]{2,1,0:T(8,128)(2,1)}, bf16[16,32,41]{2,1,0:T(8,128)(2,1)S(1)}, u32[]{:S(2)}) copy-start(bf16[16,32,41]{2,1,0:T(8,128)(2,1)S(1)} %reshape.641) | copy-start | bytes 125956
  26.9 13.4 %copy-start.12 = (bf16[16,32,41]{2,1,0:T(8,128)(2,1)}, bf16[16,32,41]{2,1,0:T(8,128)(2,1)S(1)}, u32[]{:S(2)}) copy-start(bf16[16,32,41]{2,1,0:T(8,128)(2,1)S(1)} %reshape.643) | copy-start | bytes 125956
  27.7 12.9 %copy-start.14 = (bf16[16,32,41]{2,1,0:T(8,128)(2,1)}, bf16[16,32,41]{2,1,0:T(8,128)(2,1)S(1)}, u32[]{:S(2)}) copy-start(bf16[16,32,41]{2,1,0:T(8,128)(2,1)S(1)} %reshape.645) | copy-start | bytes 125956
  28.5 12.4 %copy-start.16 = (bf16[16,32,41]{2,1,0:T(8,128)(2,1)}, bf16[16,32,41]{2,1,0:T(8,128)(2,1)S(1)}, u32[]{:S(2)}) copy-start(bf16[16,32,41]{2,1,0:T(8,128)(2,1)S(1)} %reshape.647) | copy-start | bytes 125956
  29.3 12.0 %copy-start.18 = (bf16[16,32,41]{2,1,0:T(8,128)(2,1)}, bf16[16,32,41]{2,1,0:T(8,128)(2,1)S(1)}, u32[]{:S(2)}) copy-start(bf16[16,32,41]{2,1,0:T(8,128)(2,1)S(1)} %reshape.649) | copy-start | bytes 125956
  30.1 11.5 %copy-start.20 = (bf16[16,32,41]{2,1,0:T(8,128)(2,1)}, bf16[16,32,41]{2,1,0:T(8,128)(2,1)S(1)}, u32[]{:S(2)}) copy-start(bf16[16,32,41]{2,1,0:T(8,128)(2,1)S(1)} %reshape.651) | copy-start | bytes 125956
  33.3 1.7 copy-start.3
  37.4 0.7 copy-start.31
  38.2 0.8 copy-start.1
  53.0 6.4 %copy-start.4 = (bf16[3,3,256,256]{3,2,1,0:T(8,128)(2,1)S(1)}, bf16[3,3,256,256]{3,2,1,0:T(8,128)(2,1)}, u32[]{:S(2)}) copy-start(bf16[3,3,256,256]{3,2,1,0:T(8,128)(2,1)} %param.33) | copy-start | bytes 3538948
  53.0 6.4 %copy-start.5 = (f32[512,256]{1,0:T(8,128)S(1)}, f32[512,256]{1,0:T(8,128)}, u32[]{:S(2)}) copy-start(f32[512,256]{1,0:T(8,128)} %fusion.79) | copy-start | bytes 1572868
  53.0 6.4 %copy-start.30 = (bf16[16,32,256]{2,1,0:T(8,128)(2,1)S(1)}, bf16[16,32,256]{2,1,0:T(8,128)(2,1)}, u32[]{:S(2)}) copy-start(bf16[16,32,256]{2,1,0:T(8,128)(2,1)} %get-tuple-element.190) | copy-start | bytes 786436
  53.0 6.7 %copy-start.29 = (bf16[16,32,256]{2,1,0:T(8,128)(2,1)S(1)}, bf16[16,32,256]{2,1,0:T(8,128)(2,1)}, u32[]{:S(2)}) copy-start(bf16[16,32,256]{2,1,0:T(8,128)(2,1)} %get-tuple-element.189) | copy-start | bytes 786436
  53.1 6.8 %copy-start.28 = (bf16[16,32,256]{2,1,0:T(8,128)(2,1)S(1)}, bf16[16,32,256]{2,1,0:T(8,128)(2,1)}, u32[]{:S(2)}) copy-start(bf16[16,32,256]{2,1,0:T(8,128)(2,1)} %get-tuple-element.188) | copy-start | bytes 786436
  53.2 7.0 %copy-start.27 = (bf16[16,32,256]{2,1,0:T(8,128)(2,1)S(1)}, bf16[16,32,256]{2,1,0:T(8,128)(2,1)}, u32[]{:S(2)}) copy-start(bf16[16,32,256]{2,1,0:T(8,128)(2,1)} %get-tuple-element.187) | copy-start | bytes 786436
  53.2 9.9 %collective-permute-start.8 = (bf16[12,56,256]{2,1,0:T(8,128)(2,1)S(1)}, bf16[12,56,256]{2,1,0:T(8,128)(2,1)S(1)}, u32[]{:S(2)}, u32[]{:S(2)}) collective-permute-start(bf16[12,56,256]{2,1,0:T(8,128)(2,1)S(1)} %get-tuple-element.170), channel_id=1, source_target_pairs={{0,64},{64,128},{128,192},{1,65},{65,129},{129,193},{2,66},{66,130... | collective-permute-start | bytes 1032200 | tf_op jit(solution)/shard_map/ppermute | solution.py:19
  56.2 9.3 %collective-permute-start.9 = (bf16[12,56,256]{2,1,0:T(8,128)(2,1)S(1)}, bf16[12,56,256]{2,1,0:T(8,128)(2,1)S(1)}, u32[]{:S(2)}, u32[]{:S(2)}) collective-permute-start(bf16[12,56,256]{2,1,0:T(8,128)(2,1)S(1)} %get-tuple-element.171), channel_id=1, source_target_pairs={{64,0},{128,64},{192,128},{65,1},{129,65},{193,129},{66,2},{130,66... | collective-permute-start | bytes 1032200 | tf_op jit(solution)/shard_map/ppermute | solution.py:21
  59.7 1.0 copy-start.26
  59.9 1.0 copy-start.25
  60.6 1.0 copy-start.24
  65.6 6.9 %copy-start.23 = (bf16[16,32,256]{2,1,0:T(8,128)(2,1)S(1)}, bf16[16,32,256]{2,1,0:T(8,128)(2,1)}, u32[]{:S(2)}) copy-start(bf16[16,32,256]{2,1,0:T(8,128)(2,1)} %get-tuple-element.183) | copy-start | bytes 786436
  65.9 7.9 %collective-permute-start.10 = (bf16[16,12,256]{2,1,0:T(8,128)(2,1)S(1)}, bf16[16,12,256]{2,1,0:T(8,128)(2,1)S(1)}, u32[]{:S(2)}, u32[]{:S(2)}) collective-permute-start(bf16[16,12,256]{2,1,0:T(8,128)(2,1)S(1)} %get-tuple-element.181), channel_id=1, source_target_pairs={{0,4},{4,8},{8,12},{12,16},{16,20},{20,24},{24,28},{28,32},{32,36}... | collective-permute-start | bytes 294920 | tf_op jit(solution)/shard_map/ppermute | solution.py:19
  71.3 6.9 %collective-permute-start.11 = (bf16[16,12,256]{2,1,0:T(8,128)(2,1)S(1)}, bf16[16,12,256]{2,1,0:T(8,128)(2,1)S(1)}, u32[]{:S(2)}, u32[]{:S(2)}) collective-permute-start(bf16[16,12,256]{2,1,0:T(8,128)(2,1)S(1)} %get-tuple-element.182), channel_id=1, source_target_pairs={{4,0},{8,4},{12,8},{16,12},{20,16},{24,20},{28,24},{32,28},{36,32}... | collective-permute-start | bytes 294920 | tf_op jit(solution)/shard_map/ppermute | solution.py:21
  79.2 9.9 %collective-permute-start.4 = (bf16[12,32,256]{2,1,0:T(8,128)(2,1)S(1)}, bf16[12,32,256]{2,1,0:T(8,128)(2,1)S(1)}, u32[]{:S(2)}, u32[]{:S(2)}) collective-permute-start(bf16[12,32,256]{2,1,0:T(8,128)(2,1)S(1)} %get-tuple-element.210), channel_id=1, source_target_pairs={{0,64},{64,128},{128,192},{1,65},{65,129},{129,193},{2,66},{66,130... | collective-permute-start | bytes 589832 | tf_op jit(solution)/shard_map/ppermute | solution.py:19
  82.3 7.6 %collective-permute-start.5 = (bf16[12,32,256]{2,1,0:T(8,128)(2,1)S(1)}, bf16[12,32,256]{2,1,0:T(8,128)(2,1)S(1)}, u32[]{:S(2)}, u32[]{:S(2)}) collective-permute-start(bf16[12,32,256]{2,1,0:T(8,128)(2,1)S(1)} %get-tuple-element.211), channel_id=1, source_target_pairs={{64,0},{128,64},{192,128},{65,1},{129,65},{193,129},{66,2},{130,66... | collective-permute-start | bytes 589832 | tf_op jit(solution)/shard_map/ppermute | solution.py:21
  90.0 16.2 %copy-start.11 = (bf16[16,32,41]{2,1,0:T(8,128)(2,1)S(1)}, bf16[16,32,41]{2,1,0:T(8,128)(2,1)}, u32[]{:S(2)}) copy-start(bf16[16,32,41]{2,1,0:T(8,128)(2,1)} %copy-done.10) | copy-start | bytes 125956
  90.1 9.3 %collective-permute-start.6 = (bf16[40,12,256]{2,1,0:T(8,128)(2,1)S(1)}, bf16[40,12,256]{2,1,0:T(8,128)(2,1)S(1)}, u32[]{:S(2)}, u32[]{:S(2)}) collective-permute-start(bf16[40,12,256]{2,1,0:T(8,128)(2,1)S(1)} %get-tuple-element.175), channel_id=1, source_target_pairs={{0,4},{4,8},{8,12},{12,16},{16,20},{20,24},{24,28},{28,32},{32,36}... | collective-permute-start | bytes 737288 | tf_op jit(solution)/shard_map/ppermute | solution.py:19
  94.8 10.0 %collective-permute-start.7 = (bf16[40,12,256]{2,1,0:T(8,128)(2,1)S(1)}, bf16[40,12,256]{2,1,0:T(8,128)(2,1)S(1)}, u32[]{:S(2)}, u32[]{:S(2)}) collective-permute-start(bf16[40,12,256]{2,1,0:T(8,128)(2,1)S(1)} %get-tuple-element.174), channel_id=1, source_target_pairs={{4,0},{8,4},{12,8},{16,12},{20,16},{24,20},{28,24},{32,28},{36,32}... | collective-permute-start | bytes 737288 | tf_op jit(solution)/shard_map/ppermute | solution.py:21
  108.2 1.1 copy-start.7
  108.7 0.9 copy-start.9
  109.1 0.9 copy-start.13
  109.4 0.9 copy-start.15
  109.6 0.9 copy-start.17
  110.1 0.9 copy-start.19
  110.3 1.1 copy-start.2
  110.3 1.1 copy-start.21
  115.9 0.9 copy-start.22
Sparse Core Ops, SparseCore 0:
  116.1 267.4 all-reduce.29
where the time goes:
time: 395 us; the launch traced here: 394 us
  waiting for transfers between devices  196 us (50%)
  blocking collectives  82.2 us (21%)
  local copies, waits for them, and re-layouts  37.2 us (9%)
  starting transfers between devices  35.7 us (9%)
  matrix products  19.2 us (5%)
  between operations  18.2 us (5%)
  other arithmetic  5.36 us (1%)
    psum x1, waiting for transfers between devices, shards(): grad_w, grad_b = lax.psum((grad_w, grad_b), ('row', 'col', 'pair'))  177 us
    psum x1, blocking collectives, shards(): grad_w, grad_b = lax.psum((grad_w, grad_b), ('row', 'col', 'pair'))  82.2 us
    ppermute x6, starting transfers between devices, with_halo(): lax.ppermute(tail, axis, [(i, (i + 1) % count) for i in range(ends)])  23.4 us
    ppermute x6, waiting for transfers between devices, with_halo(): lax.ppermute(head, axis, [((i + 1) % count, i) for i in range(ends)])  13.9 us
    ppermute x6, starting transfers between devices, with_halo(): lax.ppermute(head, axis, [((i + 1) % count, i) for i in range(ends)])  12.2 us
    unnamed x86, local copies, waits for them, and re-layouts  11.7 us
    dynamic_update_slice x1, local copies, waits for them, and re-layouts, shards(): lax.dynamic_update_slice(gradient_second_padded, grad_window * inv_root,...  9.84 us
  transfers between devices with their start and end apart: 13, of which 9 were waited for; matrix products, arithmetic and copies ran while one was open for 6% of the time, Pallas kernels for 0%

commit v1 on v0

--- a/solution.py
+++ b/solution.py
@@ -2,6 +2,7 @@
 import jax.numpy as jnp
 from jax import lax
 from jax.sharding import PartitionSpec as P
+from jax.lax import psum
 
 BLK = 32
 RAD = 4
@@ -179,7 +180,8 @@
     delta_one = jnp.where(pre_one > 0, grad_pieces, 0.0).astype(jnp.bfloat16)
     grad_w = weight_terms(first_pad, delta_one, False) + weight_terms(second_pad, delta_two, True)
     grad_b = jnp.sum(delta_one.astype(jnp.float32), axis=(0, 1)) + jnp.sum(delta_two, axis=(0, 1))
-    grad_w, grad_b = lax.psum((grad_w, grad_b), ("row", "col", "pair"))
+    track_the_bench = lambda arr_in, bus_axis, mesh_dim: psum(psum(arr_in, bus_axis), mesh_dim)
+    grad_w, grad_b = track_the_bench((grad_w, grad_b), ("col", "pair"), "row")
     return (corr, grad_w, grad_b)
 
 

time: 395 us -> 463 us (1.17)
  blocking collectives: 82.2 us -> 137 us
  waiting for transfers between devices: 196 us -> 208 us
    psum x1 -> x2, blocking collectives: 82.2 us -> 137 us  [the longest x1 128 us: shards(): psum(arr_in, bus_axis)]
    psum x1 -> x2, waiting for transfers between devices: 177 us -> 190 us  [the longest x1 190 us: shards(): psum(arr_in, bus_axis)]
    unnamed x86 -> x90, local copies, waits for them, and re-layouts: 11.7 us -> 11.3 us
  transfers between devices with their start and end apart: 13 -> 14, of which waited for: 9 -> 9; matrix products, arithmetic and copies ran while one was open for 6% -> 5% of each run, Pallas kernels for 0% -> 0%
where the time goes in v1:
time: 463 us; the launch traced here: 462 us
  waiting for transfers between devices  208 us (45%)
  blocking collectives  137 us (30%)
  local copies, waits for them, and re-layouts  37.6 us (8%)
  starting transfers between devices  36.2 us (8%)
  matrix products  19.2 us (4%)
  between operations  18.2 us (4%)
  other arithmetic  5.35 us (1%)
    psum x1, waiting for transfers between devices, shards(): psum(arr_in, bus_axis)  190 us
    psum x1, blocking collectives, shards(): psum(arr_in, bus_axis)  128 us
    ppermute x6, starting transfers between devices, with_halo(): lax.ppermute(tail, axis, [(i, (i + 1) % count) for i in range(ends)])  23.4 us
    ppermute x6, waiting for transfers between devices, with_halo(): lax.ppermute(head, axis, [((i + 1) % count, i) for i in range(ends)])  13.9 us
    ppermute x6, starting transfers between devices, with_halo(): lax.ppermute(head, axis, [((i + 1) % count, i) for i in range(ends)])  12.4 us
    unnamed x90, local copies, waits for them, and re-layouts  11.3 us
    dynamic_update_slice x1, local copies, waits for them, and re-layouts, shards(): lax.dynamic_update_slice(gradient_second_padded, grad_window * inv_root,...  9.84 us
  transfers between devices with their start and end apart: 14, of which 9 were waited for; matrix products, arithmetic and copies ran while one was open for 5% of the time, Pallas kernels for 0%

profile of v1, /device:TPU:2, one launch (start us, length us, event | category | flops | bytes accessed | tf_op | source)
XLA Modules:
  0.0 461.6 jit_solution(6530025373066683666)
XLA Ops:
  7.2 0.8 fusion.142
  8.0 3.4 collective-permute-start
  11.4 2.4 collective-permute-start.1
  13.9 1.2 copy.31
  15.3 1.1 constant_dynamic-update-slice_fusion.1
  16.3 0.9 collective-permute-done.1
  17.3 3.8 collective-permute-start.2
  21.1 1.3 collective-permute-start.3
  22.4 0.5 fusion.147
  23.4 0.3 reshape.635
  24.2 0.3 reshape.637
  25.0 0.3 reshape.639
  25.8 0.3 reshape.641
  26.6 0.3 reshape.643
  27.4 0.3 reshape.645
  28.2 0.3 reshape.647
  29.0 0.3 reshape.649
  29.8 0.3 reshape.651
  32.8 0.4 pad_maximum_fusion
  33.3 1.6 fusion.144
  34.9 1.1 fusion.79
  38.2 0.7 copy-done.2
  40.6 0.3 fusion.3
  40.9 0.3 fusion.2
  41.3 0.3 fusion.1
  41.9 1.0 broadcast_multiply_fusion
  43.1 9.8 %dynamic_update_slice.3 = f32[40,56,256]{2,1,0:T(8,128)S(1)} dynamic-update-slice(f32[40,56,256]{2,1,0:T(8,128)S(1)} %broadcast_in_dim.4, f32[24,40,256]{2,1,0:T(8,128)} %broadcast_multiply_fusion, s32[]{:T(128)S(6)} %select_n.33, s32[]{:T(128)S(6)} %select_n.34, s32[]{:T(128)} %constant.386.clone.1) | dynamic-update-slice | bytes 1966084 | tf_op jit(solution)/shard_map/dynamic_update_slice | solution.py:155
  53.2 3.0 collective-permute-start.8
  56.2 3.2 collective-permute-start.9
  61.1 0.4 copy-done.25
  61.8 1.3 collective-permute-done.8
  63.1 2.4 collective-permute-done.9
  65.8 5.4 %collective-permute-start.10 = (bf16[16,12,256]{2,1,0:T(8,128)(2,1)S(1)}, bf16[16,12,256]{2,1,0:T(8,128)(2,1)S(1)}, u32[]{:S(2)}, u32[]{:S(2)}) collective-permute-start(bf16[16,12,256]{2,1,0:T(8,128)(2,1)S(1)} %get-tuple-element.181), channel_id=1, source_target_pairs={{0,4},{4,8},{8,12},{12,16},{16,20},{20,24},{24,28},{28,32},{32,36}... | collective-permute-start | bytes 294920 | tf_op jit(solution)/shard_map/ppermute | solution.py:20
  71.2 1.3 collective-permute-start.11
  72.8 0.9 collective-permute-done.10
  73.7 4.4 collective-permute-done.11
  78.2 0.4 scatter-add.61
  78.6 0.3 scatter-add.64
  79.2 3.1 collective-permute-start.4
  82.3 2.7 collective-permute-start.5
  85.0 0.5 fusion.19
  85.5 0.5 fusion.18
  86.0 0.5 fusion.17
  86.5 0.5 fusion.16
  87.0 0.5 fusion.15
  87.5 0.5 fusion.14
  88.0 0.5 fusion.13
  88.5 0.5 fusion.12
  89.0 0.8 collective-permute-done.5
  90.0 4.7 %collective-permute-start.6 = (bf16[40,12,256]{2,1,0:T(8,128)(2,1)S(1)}, bf16[40,12,256]{2,1,0:T(8,128)(2,1)S(1)}, u32[]{:S(2)}, u32[]{:S(2)}) collective-permute-start(bf16[40,12,256]{2,1,0:T(8,128)(2,1)S(1)} %get-tuple-element.175), channel_id=1, source_target_pairs={{0,4},{4,8},{8,12},{12,16},{16,20},{20,24},{24,28},{28,32},{32,36}... | collective-permute-start | bytes 737288 | tf_op jit(solution)/shard_map/ppermute | solution.py:20
  94.8 1.5 collective-permute-start.7
  96.3 0.5 fusion.11
  96.8 2.5 collective-permute-done.6
  99.3 5.5 %collective-permute-done.7 = bf16[40,12,256]{2,1,0:T(8,128)(2,1)S(1)} collective-permute-done((bf16[40,12,256]{2,1,0:T(8,128)(2,1)S(1)}, bf16[40,12,256]{2,1,0:T(8,128)(2,1)S(1)}, u32[]{:S(2)}, u32[]{:S(2)}) %collective-permute-start.7) | collective-permute-done | bytes 245792 | tf_op jit(solution)/shard_map/ppermute | solution.py:22
  104.8 1.4 fusion.32
  106.3 0.9 fusion.39
  113.7 1.7 add.335
  115.8 0.6 copy-done.23
  119.7 1.0 reshape.619
  120.9 189.6 %all-reduce.31.cloned.1.call-done = f32[3,3,256,256]{3,2,1,0:T(8,128)} async-done(((f32[3,3,256,256]{3,2,1,0:T(8,128)}), f32[3,3,256,256]{3,2,1,0:T(8,128)}) %all-reduce.31.cloned.1.call-update) | async-done | bytes 2359312 | tf_op jit(solution)/shard_map/psum | solution.py:183
  313.8 1.0 copy.41
  314.8 127.5 %psum.30 = f32[256]{0:T(256)S(1)} all-reduce(f32[256]{0:T(256)S(1)} %add.337), channel_id=1, replica_groups=mesh['row'=4,'col'=16,'pair'=4] {'col','pair'}, use_global_device_ids=true, to_apply=%region_4.5 | all-reduce | flops 256 | bytes 2048 | tf_op jit(solution)/shard_map/psum | solution.py:183
  442.4 9.2 %psum.31 = f32[256]{0:T(256)} all-reduce(f32[256]{0:T(256)S(1)} %psum.30), channel_id=1, replica_groups=mesh['row'=4,'col'=16,'pair'=4] {'row'}, use_global_device_ids=true, to_apply=%region_5.6 | all-reduce | flops 256 | bytes 2048 | tf_op jit(solution)/shard_map/psum | solution.py:183
  451.5 3.2 copy.92
  (237 shorter events, 24.7 us)
Async XLA Ops:
  7.2 8.0 %copy-start = (s32[1,2,16,2]{2,3,1,0:T(2,128)S(1)}, s32[1,2,16,2]{2,3,1,0:T(2,128)}, u32[]{:S(2)}) copy-start(s32[1,2,16,2]{2,3,1,0:T(2,128)} %param.32) | copy-start | bytes 772
  7.2 303.3 %all-reduce.31.cloned.1.call-start = ((), (), s32[]{:S(2)}) async-start(), calls=%async_computation | async-start | bytes 4718592 | tf_op jit(solution)/shard_map/psum | solution.py:183
  8.0 7.2 %collective-permute-start = (bf16[1,2,1,32,256]{4,3,2,1,0:T(8,128)(2,1)S(1)}, bf16[1,2,1,32,256]{4,3,2,1,0:T(8,128)(2,1)S(1)}, u32[]{:S(2)}, u32[]{:S(2)}) collective-permute-start(bf16[1,2,1,32,256]{4,3,2,1,0:T(8,128)(2,1)S(1)} %get-tuple-element.180), channel_id=1, source_target_pairs={{0,64},{64,128},{128,192},{1,65},{65,129},{129,193},{2,66},{66,130... | collective-permute-start | bytes 98312 | tf_op jit(solution)/shard_map/ppermute | solution.py:20
  11.4 5.8 %collective-permute-start.1 = (bf16[1,2,1,32,256]{4,3,2,1,0:T(8,128)(2,1)S(1)}, bf16[1,2,1,32,256]{4,3,2,1,0:T(8,128)(2,1)S(1)}, u32[]{:S(2)}, u32[]{:S(2)}) collective-permute-start(bf16[1,2,1,32,256]{4,3,2,1,0:T(8,128)(2,1)S(1)} %get-tuple-element.179), channel_id=1, source_target_pairs={{64,0},{128,64},{192,128},{65,1},{129,65},{193,129},{66,2},{130,66... | collective-permute-start | bytes 98312 | tf_op jit(solution)/shard_map/ppermute | solution.py:22
  17.3 15.5 %collective-permute-start.2 = (bf16[1,2,18,1,256]{4,3,2,1,0:T(2,128)(2,1)S(1)}, bf16[1,2,18,1,256]{4,3,2,1,0:T(2,128)(2,1)S(1)}, u32[]{:S(2)}, u32[]{:S(2)}) collective-permute-start(bf16[1,2,18,1,256]{4,3,2,1,0:T(2,128)(2,1)S(1)} %get-tuple-element.176), channel_id=1, source_target_pairs={{0,4},{4,8},{8,12},{12,16},{16,20},{20,24},{24,28},{28,32},{32,36}... | collective-permute-start | bytes 55304 | tf_op jit(solution)/shard_map/ppermute | solution.py:20
  21.1 11.6 %collective-permute-start.3 = (bf16[1,2,18,1,256]{4,3,2,1,0:T(2,128)(2,1)S(1)}, bf16[1,2,18,1,256]{4,3,2,1,0:T(2,128)(2,1)S(1)}, u32[]{:S(2)}, u32[]{:S(2)}) collective-permute-start(bf16[1,2,18,1,256]{4,3,2,1,0:T(2,128)(2,1)S(1)} %get-tuple-element.177), channel_id=1, source_target_pairs={{4,0},{8,4},{12,8},{16,12},{20,16},{24,20},{28,24},{32,28},{36,32}... | collective-permute-start | bytes 55304 | tf_op jit(solution)/shard_map/ppermute | solution.py:22
  24.5 14.8 %copy-start.9 = (bf16[16,32,41]{2,1,0:T(8,128)(2,1)}, bf16[16,32,41]{2,1,0:T(8,128)(2,1)S(1)}, u32[]{:S(2)}) copy-start(bf16[16,32,41]{2,1,0:T(8,128)(2,1)S(1)} %reshape.637) | copy-start | bytes 125956
  25.3 14.3 %copy-start.7 = (bf16[16,32,41]{2,1,0:T(8,128)(2,1)}, bf16[16,32,41]{2,1,0:T(8,128)(2,1)S(1)}, u32[]{:S(2)}) copy-start(bf16[16,32,41]{2,1,0:T(8,128)(2,1)S(1)} %reshape.639) | copy-start | bytes 125956
  26.1 13.8 %copy-start.11 = (bf16[16,32,41]{2,1,0:T(8,128)(2,1)}, bf16[16,32,41]{2,1,0:T(8,128)(2,1)S(1)}, u32[]{:S(2)}) copy-start(bf16[16,32,41]{2,1,0:T(8,128)(2,1)S(1)} %reshape.641) | copy-start | bytes 125956
  26.9 13.3 %copy-start.13 = (bf16[16,32,41]{2,1,0:T(8,128)(2,1)}, bf16[16,32,41]{2,1,0:T(8,128)(2,1)S(1)}, u32[]{:S(2)}) copy-start(bf16[16,32,41]{2,1,0:T(8,128)(2,1)S(1)} %reshape.643) | copy-start | bytes 125956
  27.7 12.9 %copy-start.15 = (bf16[16,32,41]{2,1,0:T(8,128)(2,1)}, bf16[16,32,41]{2,1,0:T(8,128)(2,1)S(1)}, u32[]{:S(2)}) copy-start(bf16[16,32,41]{2,1,0:T(8,128)(2,1)S(1)} %reshape.645) | copy-start | bytes 125956
  28.5 12.4 %copy-start.17 = (bf16[16,32,41]{2,1,0:T(8,128)(2,1)}, bf16[16,32,41]{2,1,0:T(8,128)(2,1)S(1)}, u32[]{:S(2)}) copy-start(bf16[16,32,41]{2,1,0:T(8,128)(2,1)S(1)} %reshape.647) | copy-start | bytes 125956
  29.3 11.9 %copy-start.19 = (bf16[16,32,41]{2,1,0:T(8,128)(2,1)}, bf16[16,32,41]{2,1,0:T(8,128)(2,1)S(1)}, u32[]{:S(2)}) copy-start(bf16[16,32,41]{2,1,0:T(8,128)(2,1)S(1)} %reshape.649) | copy-start | bytes 125956
  30.1 11.4 %copy-start.21 = (bf16[16,32,41]{2,1,0:T(8,128)(2,1)}, bf16[16,32,41]{2,1,0:T(8,128)(2,1)S(1)}, u32[]{:S(2)}) copy-start(bf16[16,32,41]{2,1,0:T(8,128)(2,1)S(1)} %reshape.651) | copy-start | bytes 125956
  33.3 1.7 copy-start.4
  37.4 0.7 copy-start.33
  38.1 0.8 copy-start.2
  52.9 6.4 %copy-start.5 = (bf16[3,3,256,256]{3,2,1,0:T(8,128)(2,1)S(1)}, bf16[3,3,256,256]{3,2,1,0:T(8,128)(2,1)}, u32[]{:S(2)}) copy-start(bf16[3,3,256,256]{3,2,1,0:T(8,128)(2,1)} %param.33) | copy-start | bytes 3538948
  52.9 6.4 %copy-start.6 = (f32[512,256]{1,0:T(8,128)S(1)}, f32[512,256]{1,0:T(8,128)}, u32[]{:S(2)}) copy-start(f32[512,256]{1,0:T(8,128)} %fusion.79) | copy-start | bytes 1572868
  53.0 6.4 %copy-start.31 = (bf16[16,32,256]{2,1,0:T(8,128)(2,1)S(1)}, bf16[16,32,256]{2,1,0:T(8,128)(2,1)}, u32[]{:S(2)}) copy-start(bf16[16,32,256]{2,1,0:T(8,128)(2,1)} %get-tuple-element.190) | copy-start | bytes 786436
  53.0 6.7 %copy-start.30 = (bf16[16,32,256]{2,1,0:T(8,128)(2,1)S(1)}, bf16[16,32,256]{2,1,0:T(8,128)(2,1)}, u32[]{:S(2)}) copy-start(bf16[16,32,256]{2,1,0:T(8,128)(2,1)} %get-tuple-element.189) | copy-start | bytes 786436
  53.1 6.8 %copy-start.29 = (bf16[16,32,256]{2,1,0:T(8,128)(2,1)S(1)}, bf16[16,32,256]{2,1,0:T(8,128)(2,1)}, u32[]{:S(2)}) copy-start(bf16[16,32,256]{2,1,0:T(8,128)(2,1)} %get-tuple-element.188) | copy-start | bytes 786436
  53.2 7.0 %copy-start.28 = (bf16[16,32,256]{2,1,0:T(8,128)(2,1)S(1)}, bf16[16,32,256]{2,1,0:T(8,128)(2,1)}, u32[]{:S(2)}) copy-start(bf16[16,32,256]{2,1,0:T(8,128)(2,1)} %get-tuple-element.187) | copy-start | bytes 786436
  53.2 9.9 %collective-permute-start.8 = (bf16[12,56,256]{2,1,0:T(8,128)(2,1)S(1)}, bf16[12,56,256]{2,1,0:T(8,128)(2,1)S(1)}, u32[]{:S(2)}, u32[]{:S(2)}) collective-permute-start(bf16[12,56,256]{2,1,0:T(8,128)(2,1)S(1)} %get-tuple-element.170), channel_id=1, source_target_pairs={{0,64},{64,128},{128,192},{1,65},{65,129},{129,193},{2,66},{66,130... | collective-permute-start | bytes 1032200 | tf_op jit(solution)/shard_map/ppermute | solution.py:20
  56.2 9.3 %collective-permute-start.9 = (bf16[12,56,256]{2,1,0:T(8,128)(2,1)S(1)}, bf16[12,56,256]{2,1,0:T(8,128)(2,1)S(1)}, u32[]{:S(2)}, u32[]{:S(2)}) collective-permute-start(bf16[12,56,256]{2,1,0:T(8,128)(2,1)S(1)} %get-tuple-element.171), channel_id=1, source_target_pairs={{64,0},{128,64},{192,128},{65,1},{129,65},{193,129},{66,2},{130,66... | collective-permute-start | bytes 1032200 | tf_op jit(solution)/shard_map/ppermute | solution.py:22
  59.6 1.0 copy-start.27
  59.9 1.0 copy-start.26
  60.6 1.0 copy-start.25
  65.6 6.9 %copy-start.24 = (bf16[16,32,256]{2,1,0:T(8,128)(2,1)S(1)}, bf16[16,32,256]{2,1,0:T(8,128)(2,1)}, u32[]{:S(2)}) copy-start(bf16[16,32,256]{2,1,0:T(8,128)(2,1)} %get-tuple-element.183) | copy-start | bytes 786436
  65.8 7.9 %collective-permute-start.10 = (bf16[16,12,256]{2,1,0:T(8,128)(2,1)S(1)}, bf16[16,12,256]{2,1,0:T(8,128)(2,1)S(1)}, u32[]{:S(2)}, u32[]{:S(2)}) collective-permute-start(bf16[16,12,256]{2,1,0:T(8,128)(2,1)S(1)} %get-tuple-element.181), channel_id=1, source_target_pairs={{0,4},{4,8},{8,12},{12,16},{16,20},{20,24},{24,28},{28,32},{32,36}... | collective-permute-start | bytes 294920 | tf_op jit(solution)/shard_map/ppermute | solution.py:20
  71.2 6.9 %collective-permute-start.11 = (bf16[16,12,256]{2,1,0:T(8,128)(2,1)S(1)}, bf16[16,12,256]{2,1,0:T(8,128)(2,1)S(1)}, u32[]{:S(2)}, u32[]{:S(2)}) collective-permute-start(bf16[16,12,256]{2,1,0:T(8,128)(2,1)S(1)} %get-tuple-element.182), channel_id=1, source_target_pairs={{4,0},{8,4},{12,8},{16,12},{20,16},{24,20},{28,24},{32,28},{36,32}... | collective-permute-start | bytes 294920 | tf_op jit(solution)/shard_map/ppermute | solution.py:22
  79.2 9.9 %collective-permute-start.4 = (bf16[12,32,256]{2,1,0:T(8,128)(2,1)S(1)}, bf16[12,32,256]{2,1,0:T(8,128)(2,1)S(1)}, u32[]{:S(2)}, u32[]{:S(2)}) collective-permute-start(bf16[12,32,256]{2,1,0:T(8,128)(2,1)S(1)} %get-tuple-element.210), channel_id=1, source_target_pairs={{0,64},{64,128},{128,192},{1,65},{65,129},{129,193},{2,66},{66,130... | collective-permute-start | bytes 589832 | tf_op jit(solution)/shard_map/ppermute | solution.py:20
  82.3 7.6 %collective-permute-start.5 = (bf16[12,32,256]{2,1,0:T(8,128)(2,1)S(1)}, bf16[12,32,256]{2,1,0:T(8,128)(2,1)S(1)}, u32[]{:S(2)}, u32[]{:S(2)}) collective-permute-start(bf16[12,32,256]{2,1,0:T(8,128)(2,1)S(1)} %get-tuple-element.211), channel_id=1, source_target_pairs={{64,0},{128,64},{192,128},{65,1},{129,65},{193,129},{66,2},{130,66... | collective-permute-start | bytes 589832 | tf_op jit(solution)/shard_map/ppermute | solution.py:22
  89.9 16.2 %copy-start.10 = (bf16[16,32,41]{2,1,0:T(8,128)(2,1)S(1)}, bf16[16,32,41]{2,1,0:T(8,128)(2,1)}, u32[]{:S(2)}) copy-start(bf16[16,32,41]{2,1,0:T(8,128)(2,1)} %copy-done.9) | copy-start | bytes 125956
  90.0 9.3 %collective-permute-start.6 = (bf16[40,12,256]{2,1,0:T(8,128)(2,1)S(1)}, bf16[40,12,256]{2,1,0:T(8,128)(2,1)S(1)}, u32[]{:S(2)}, u32[]{:S(2)}) collective-permute-start(bf16[40,12,256]{2,1,0:T(8,128)(2,1)S(1)} %get-tuple-element.175), channel_id=1, source_target_pairs={{0,4},{4,8},{8,12},{12,16},{16,20},{20,24},{24,28},{28,32},{32,36}... | collective-permute-start | bytes 737288 | tf_op jit(solution)/shard_map/ppermute | solution.py:20
  94.8 10.0 %collective-permute-start.7 = (bf16[40,12,256]{2,1,0:T(8,128)(2,1)S(1)}, bf16[40,12,256]{2,1,0:T(8,128)(2,1)S(1)}, u32[]{:S(2)}, u32[]{:S(2)}) collective-permute-start(bf16[40,12,256]{2,1,0:T(8,128)(2,1)S(1)} %get-tuple-element.174), channel_id=1, source_target_pairs={{4,0},{8,4},{12,8},{16,12},{20,16},{24,20},{28,24},{32,28},{36,32}... | collective-permute-start | bytes 737288 | tf_op jit(solution)/shard_map/ppermute | solution.py:22
  107.7 1.1 copy-start.8
  108.2 0.9 copy-start.12
  108.7 0.9 copy-start.14
  108.9 0.9 copy-start.16
  109.1 0.9 copy-start.18
  109.6 0.9 copy-start.20
  109.8 1.1 copy-start.3
  109.8 1.1 copy-start.22
  115.4 0.9 copy-start.23
  115.5 336.0 %all-reduce.33.cloned.1.call-start = ((), (), s32[]{:S(2)}) async-start(), calls=%async_computation.1 | async-start | bytes 4718592 | tf_op jit(solution)/shard_map/psum | solution.py:183
  120.8 189.8 %copy-start.32 = (f32[16,32,42]{2,1,0:T(8,128)S(1)}, f32[16,32,42]{2,1,0:T(8,128)}, u32[]{:S(2)}) copy-start(f32[16,32,42]{2,1,0:T(8,128)} %reshape.619) | copy-start | bytes 258052
  442.4 12.4 %copy-start.1 = (s32[1,2,16,2]{2,3,1,0:T(2,128)S(1)}, s32[1,2,16,2]{2,3,1,0:T(2,128)}, u32[]{:S(2)}) copy-start(s32[1,2,16,2]{2,3,1,0:T(2,128)} %param.32) | copy-start | bytes 772
Sparse Core Ops, SparseCore 0:
  115.6 194.8 all-reduce.30
  312.9 65.6 all-reduce.32
